TPU v7x, 32 devices: a whole 2x2x4 slice. The times are simulated.
32 devices in a mesh: tp: 2 (over y), req: 16 (over z, x, core).
Axes of the slice: x: 2, y: 2, z: 4, core: 2. Of those that a mesh axis runs over, the one named last changes fastest.
Arguments:
- token_ids: int32 [8192], P('req'), may hold values from 0 to 31999, as said below
- prompt_lengths: int32 [16, 4], P('req'), may hold values from 1 to 256, 512 in all within a row
- tenant_ids: int32 [16, 4], P('req'), may hold values from 0 to 1, never falling along the last dimension, each value on 1 to 3 neighbouring positions
- embed_table: bfloat16 [32000, 1536], P('req'), may hold values from -6 to 6
- attention_gain: float32 [1536], replicated, may hold values from 0.1 to 1.9
- qkv_weight: float32 [1536, 3072], P(('tp', 'req')), may hold values from -0.25 to 0.25
- out_weight: bfloat16 [1536, 1536], P('tp'), may hold values from -0.15625 to 0.15625
- ffn_gain: float32 [1536], replicated, may hold values from 0.1 to 1.9
- gate_up_weight: float32 [1536, 8192], P(('tp', 'req')), may hold values from -0.15625 to 0.15625
- down_weight: bfloat16 [4096, 1536], P('tp'), may hold values from -0.09375 to 0.09375
Outputs:
- final_hidden: bfloat16 [8192, 1536], P('req')
- kv_cache: bfloat16 [2, 8192, 768], P(None, 'req', 'tp')
Inputs may be any that keep to these rules, and one draw needn't show every extreme that they name: Split token_ids into aligned blocks of 256 tokens and the ids into ranges of 2000 consecutive ids: no block has more than 32 ids in one range, and one range gets exactly 32 ids from every block. `prompt_lengths`: the 4 lengths of a request group sum to 512. `tenant_ids`: never falling along the prompts of a request group; every tenant has one to 3 prompts.
All inputs are finite; a program needn't handle non-finite values.
Results may differ from a plain program's by a relative error of at most 0.01.
Values may be sent and summed in bfloat16 or wider, within the bound.
No kernel may reach another device: no remote copies, remote signals or barrier semaphores. Data moves between devices by JAX's collectives and lax.ppermute only.
A program may use at most 128 MiB of HBM per device.

v0:
```python
import jax
import jax.numpy as jnp
from jax import lax
from jax.sharding import PartitionSpec as P

HEAD_DIM = 96
rope_base = 100000.0
norm_eps = 1e-05


def rms_scaled(values, gain):
    mean_square = jnp.mean(values * values, axis=-1, keepdims=True)
    return (values * lax.rsqrt(mean_square + norm_eps) * gain).astype(jnp.bfloat16)


def token_layout(lengths, tenants, row_count):
    positions = jnp.arange(row_count, dtype=jnp.int32)
    prompt_ends = jnp.cumsum(lengths)
    prompt_starts = prompt_ends - lengths
    passed = (positions[:, None] >= prompt_ends[None, :]).astype(jnp.int32)
    prompt = jnp.sum(passed, axis=1)
    in_prompt = (prompt[:, None] == jnp.arange(lengths.shape[0], dtype=jnp.int32)[None, :]).astype(
        jnp.int32
    )
    offset = positions - jnp.sum(in_prompt * prompt_starts[None, :], axis=1)
    tenant = jnp.sum(in_prompt * tenants[None, :], axis=1)
    return (offset, tenant)


def rotate(values, offset):
    half_dim = values.shape[-1] // 2
    frequency = rope_base ** (-2.0 * jnp.arange(half_dim, dtype=jnp.float32) / values.shape[-1])
    angles = offset.astype(jnp.float32)[:, None] * frequency[None, :]
    cosine = jnp.cos(angles)[:, None, :]
    sine_part = jnp.sin(angles)[:, None, :]
    lower_half = values[..., :half_dim]
    upper_half = values[..., half_dim:]
    return jnp.concatenate(
        [
            lower_half * cosine - upper_half * sine_part,
            upper_half * cosine + lower_half * sine_part,
        ],
        axis=-1,
    )


def attend(queries, key_heads, value_heads, tenant):
    row_count = queries.shape[0]
    positions = jnp.arange(row_count, dtype=jnp.int32)
    score_scale = queries.shape[-1] ** (-0.5)
    allowed = (positions[None, :] <= positions[:, None]) & (tenant[None, :] == tenant[:, None])
    scores = (
        jnp.einsum("qkgd,skd->kgqs", queries, key_heads, preferred_element_type=jnp.float32)
        * score_scale
    )
    scores = jnp.where(allowed[None, None], scores, -jnp.inf)
    row_max = jnp.max(scores, axis=-1, keepdims=True)
    expo = jnp.exp(scores - row_max)
    weights = (expo / jnp.sum(expo, axis=-1, keepdims=True)).astype(jnp.bfloat16)
    mixed_out = jnp.einsum(
        "kgqs,skd->qkgd", weights, value_heads, preferred_element_type=jnp.float32
    )
    pieces = mixed_out.astype(jnp.bfloat16)
    return pieces


def ffn_hidden(normed_ffn, gate_cols, ff_half):
    gate_up = jnp.dot(normed_ffn, gate_cols, preferred_element_type=jnp.float32)
    return (jax.nn.silu(gate_up[:, :ff_half]) * gate_up[:, ff_half:]).astype(jnp.bfloat16)


def per_device(
    token_ids,
    prompt_lengths,
    tenant_ids,
    embed_table,
    attention_gain,
    qkv_weight,
    out_weight,
    ffn_gain,
    gate_up_weight,
    down_weight,
):
    tp_count = lax.axis_size("tp")
    tp_index = lax.axis_index("tp")
    group_count = lax.axis_size("req")
    tokens = token_ids.shape[0]
    looked = tokens // tp_count
    own_rows = embed_table.shape[0]
    capacity = max(2, 2 * looked // group_count)
    my_ids = lax.dynamic_slice_in_dim(token_ids, tp_index * looked, looked)
    owner_of = my_ids // own_rows
    row_in_range = my_ids - owner_of * own_rows
    owner_hits = (owner_of[:, None] == jnp.arange(group_count, dtype=jnp.int32)[None, :]).astype(
        jnp.int32
    )
    slot_of = jnp.sum((jnp.cumsum(owner_hits, axis=0) - owner_hits) * owner_hits, axis=1)
    requests = (
        jnp.full((group_count, capacity), -1, jnp.int32).at[owner_of, slot_of].set(row_in_range)
    )
    found_rows = jnp.take(
        embed_table,
        jnp.maximum(lax.all_to_all(requests, "req", split_axis=0, concat_axis=0, tiled=True), 0),
        axis=0,
    )
    returned = lax.all_to_all(found_rows, "req", split_axis=0, concat_axis=0, tiled=True)
    embedded = lax.all_gather(returned[owner_of, slot_of], "tp", axis=0, tiled=True)
    offset, tenant = token_layout(prompt_lengths[0], tenant_ids[0], tokens)
    rows_here = qkv_weight.shape[0]
    q_half = out_weight.shape[0]
    ff_half = down_weight.shape[0]
    q_full = q_half * tp_count
    kv_half = (qkv_weight.shape[1] - q_full) // (2 * tp_count)
    kv_full = kv_half * tp_count
    packed = qkv_weight.astype(jnp.bfloat16)
    gate_up_bf = gate_up_weight.astype(jnp.bfloat16)
    packed_rows = jnp.concatenate(
        [
            packed[:, :q_full].reshape(rows_here, tp_count, q_half),
            packed[:, q_full : q_full + kv_full].reshape(rows_here, tp_count, kv_half),
            packed[:, q_full + kv_full :].reshape(rows_here, tp_count, kv_half),
            gate_up_bf.reshape(rows_here, 2, tp_count, ff_half)
            .transpose(0, 2, 1, 3)
            .reshape(rows_here, tp_count, 2 * ff_half),
        ],
        axis=2,
    )
    collected = lax.all_gather(packed_rows, "req", axis=0, tiled=True)
    columns = lax.all_to_all(collected, "tp", split_axis=1, concat_axis=0, tiled=True)
    weights = columns[:, 0, :]
    normed = rms_scaled(embedded.astype(jnp.float32), attention_gain)
    projected = jnp.dot(
        normed, weights[:, : q_half + 2 * kv_half], preferred_element_type=jnp.float32
    )
    kv_local = kv_half // HEAD_DIM
    queries = rotate(
        projected[:, :q_half].reshape(tokens, q_half // HEAD_DIM, HEAD_DIM), offset
    ).astype(jnp.bfloat16)
    key_heads = rotate(
        projected[:, q_half : q_half + kv_half].reshape(tokens, kv_local, HEAD_DIM), offset
    ).astype(jnp.bfloat16)
    value_heads = (
        projected[:, q_half + kv_half :].reshape(tokens, kv_local, HEAD_DIM).astype(jnp.bfloat16)
    )
    kv_cache = jnp.stack([key_heads.reshape(tokens, kv_half), value_heads.reshape(tokens, kv_half)])
    attended = attend(
        queries.reshape(tokens, kv_local, -1, HEAD_DIM), key_heads, value_heads, tenant
    ).reshape(tokens, q_half)
    gate_cols = weights[:, q_half + 2 * kv_half :]
    attn_sum = lax.psum(
        jnp.dot(attended, out_weight, preferred_element_type=jnp.float32).astype(jnp.bfloat16), "tp"
    ).astype(jnp.float32)
    residual = embedded.astype(jnp.float32) + attn_sum
    normed_ffn = rms_scaled(residual, ffn_gain)
    hidden = ffn_hidden(normed_ffn, gate_cols, ff_half)
    ffn_sum = lax.psum(
        jnp.dot(hidden, down_weight, preferred_element_type=jnp.float32).astype(jnp.bfloat16), "tp"
    ).astype(jnp.float32)
    final_out = (residual + ffn_sum).astype(jnp.bfloat16)
    return (final_out, kv_cache)


def solution(mesh):
    return jax.shard_map(
        per_device,
        mesh=mesh,
        in_specs=(
            P("req"),
            P("req", None),
            P("req", None),
            P("req", None),
            P(),
            P(("tp", "req"), None),
            P("tp", None),
            P(),
            P(("tp", "req"), None),
            P("tp", None),
        ),
        out_specs=(P("req", None), P(None, "req", "tp")),
        check_vma=False,
    )
```

profile of v0, /device:TPU:0, one launch (start us, length us, event | category | flops | bytes accessed | tf_op | source)
XLA Modules:
  0.0 530.0 jit_solution(3900098590027576408)
XLA Ops:
  8.1 1.2 convert_element_type.91
  9.3 2.4 convert_element_type.92
  11.7 2.6 reshape.236
  14.3 1.5 copy.85
  15.8 2.5 reshape.237
  20.5 12.8 %scatter_fusion = s32[16,32]{1,0:T(8,128)S(1)} fusion(s32[16,32]{1,0:T(8,128)S(1)} %broadcast_in_dim.22, s32[256]{0:T(256)S(1)} %bitcast.107, s32[256]{0:T(256)S(1)} %get-tuple-element.4), kind=kCustom, calls=%fused_computation.2 | custom fusion | bytes 5120 | tf_op jit(solution)/shard_map/scatter | solution.py:99
  33.3 13.7 %all_to_all.29 = s32[16,1,32]{2,1,0:T(1,128)S(1)} all-to-all(s32[16,1,32]{2,1,0:T(1,128)S(1)} %bitcast.105), channel_id=1, replica_groups=mesh['tp'=2,'req'=16] {'req'}, dimensions={0} | all-to-all | bytes 4096 | tf_op jit(solution)/shard_map/all_to_all | solution.py:103
  47.0 8.0 %gather_fusion = bf16[512,1536]{1,0:T(8,128)(2,1)} fusion(bf16[2000,1536]{1,0:T(8,128)(2,1)} %param.13, s32[1024]{0:T(1024)S(1)} %pad_clamp_fusion), kind=kCustom, calls=%fused_computation | custom fusion | bytes 3147776 | tf_op jit(solution)/shard_map/jit(_take)/gather | solution.py:101
  55.0 1.7 broadcast_select_fusion
  56.7 60.0 %all_to_all.30 = bf16[16,32,1536]{2,1,0:T(8,128)(2,1)} all-to-all(bf16[16,32,1536]{2,1,0:T(8,128)(2,1)S(1)} %broadcast_select_fusion), channel_id=1, replica_groups=mesh['tp'=2,'req'=16] {'req'}, dimensions={0} | all-to-all | bytes 3145728 | tf_op jit(solution)/shard_map/all_to_all | solution.py:106
  116.7 25.0 %all-gather.5.cloned.1.call-done = bf16[768,2,5632]{2,0,1:T(8,128)(2,1)} async-done(((bf16[48,2,5632]{2,0,1:T(8,128)(2,1)}), bf16[768,2,5632]{2,0,1:T(8,128)(2,1)}) %all-gather.5.cloned.1.call-update) | async-done | bytes 17301520 | tf_op jit(solution)/shard_map/all_gather | solution.py:128
  141.7 9.8 %all-to-all-start.2 = ((bf16[768,2,5632]{2,0,1:T(8,128)(2,1)}), bf16[768,2,5632]{2,0,1:T(8,128)(2,1)}, u32[]{:S(2)}, u32[]{:S(2)}) async-start(bf16[768,2,5632]{2,0,1:T(8,128)(2,1)} %all-gather.5.cloned.1.call-done), calls=%async_computation.2 | async-start | bytes 34603008 | tf_op jit(solution)/shard_map/all_to_all | solution.py:129
  151.6 4.6 gather_fusion.1
  158.9 47.1 %all-gather.3.cloned.1.call-done = bf16[512,1536]{1,0:T(8,128)(2,1)} async-done(((bf16[256,1536]{1,0:T(8,128)(2,1)}), bf16[512,1536]{1,0:T(8,128)(2,1)}) %all-gather.3.cloned.1.call-update) | async-done | bytes 1572880 | tf_op jit(solution)/shard_map/all_gather | solution.py:107
  206.0 1.8 fusion.11
  207.8 149.1 %all-to-all-done.2 = bf16[768,2,5632]{2,0,1:T(8,128)(2,1)} async-done(((bf16[768,2,5632]{2,0,1:T(8,128)(2,1)}), bf16[768,2,5632]{2,0,1:T(8,128)(2,1)}, u32[]{:S(2)}, u32[]{:S(2)}) %all-to-all-start.2) | async-done | bytes 17301536 | tf_op jit(solution)/shard_map/all_to_all | solution.py:129
  356.9 5.0 fusion.4
  362.0 1.4 slice.79
  365.1 3.1 copy.70
  368.3 1.1 copy.69
  369.5 2.4 subtract_convert_fusion
  371.8 1.2 multiply_subtract_fusion
  373.1 7.4 %fusion.44 = (f32[4,2,512]{2,1,0:T(2,128)S(1)}, f32[4,2,512,512]{2,3,1,0:T(8,128)}) fusion(pred[512,512]{0,1:T(8,128)(4,1)} %fusion.21, bf16[512,4,2,48]{0,3,2,1:T(8,128)(2,1)} %bitcast.117, bf16[512,4,2,48]{0,3,2,1:T(8,128)(2,1)S(1)} %bitcast.116, bf16[512,4,48]{0,2,1:T(8,128)(2,1)S(1)} %get-tuple-element.11, bf16[512,4,48]{0,2,1:T(8,128)(2,1)S(1)} %get-tuple-element.10), kind=kOutput, calls=%fused_computation.93 | convolution fusion | flops 413401600 | bytes 9846784 | tf_op jit(solution)/shard_map/sub | solution.py:58
  380.5 4.2 fusion.20
  384.7 2.6 convolution_convert_fusion.1
  387.6 55.3 %all-reduce.3.cloned.1.call-done = bf16[512,1536]{1,0:T(8,128)(2,1)} async-done(((bf16[512,1536]{1,0:T(8,128)(2,1)}), bf16[512,1536]{1,0:T(8,128)(2,1)}) %all-reduce.3.cloned.1.call-update) | async-done | bytes 1572880 | tf_op jit(solution)/shard_map/psum | solution.py:150
  442.9 2.6 multiply_reduce_fusion
  445.7 12.1 %fusion.1 = f32[512,4096]{1,0:T(8,128)} fusion(bf16[1536,5632]{1,0:T(8,128)(2,1)} %bitcast.14, bf16[512,1536]{1,0:T(8,128)(2,1)S(1)} %copy-done.2, bf16[512,1536]{1,0:T(8,128)(2,1)S(1)} %copy-done.1, f32[1536]{0:T(1024)S(1)} %copy-done.10, f32[512]{0:T(512)S(1)} %add_rsqrt_fusion), kind=kOutput, calls=%fused_computation.4 | convolution fusion | flops 6447169536 | bytes 24125440 | tf_op jit(solution)/shard_map/dot_general | solution.py:68
  457.8 9.1 %convolution_convert_fusion = bf16[512,1536]{1,0:T(8,128)(2,1)} fusion(bf16[2048,1536]{1,0:T(8,128)(2,1)S(1)} %bitcast.129, f32[512,4096]{1,0:T(8,128)} %fusion.1), kind=kOutput, calls=%fused_computation.27 | convolution fusion | flops 3228303360 | bytes 16252928 | tf_op jit(solution)/shard_map/dot_general | solution.py:157
  467.2 1.2 slice_bitcast_fusion
  469.4 49.0 %all-reduce.5.cloned.1.call-done = bf16[512,1536]{1,0:T(8,128)(2,1)} async-done(((bf16[512,1536]{1,0:T(8,128)(2,1)}), bf16[512,1536]{1,0:T(8,128)(2,1)}) %all-reduce.5.cloned.1.call-update) | async-done | bytes 1572880 | tf_op jit(solution)/shard_map/psum | solution.py:156
  518.3 4.1 add_convert_fusion
  (73 shorter events, 8.5 us)
Async XLA Ops:
  8.0 376.7 %copy-start = (bf16[768,1536]{1,0:T(8,128)(2,1)S(1)}, bf16[768,1536]{1,0:T(8,128)(2,1)}, u32[]{:S(2)}) copy-start(bf16[768,1536]{1,0:T(8,128)(2,1)} %param.16) | copy-start | bytes 7077892
  8.0 133.7 %all-gather.5.cloned.1.call-start = ((), (), s32[]{:S(2)}) async-start(), calls=%async_computation.4 | async-start | bytes 18382848 | tf_op jit(solution)/shard_map/all_gather | solution.py:128
  14.3 5.2 copy-start.8
  141.7 215.2 %all-to-all-start.2 = ((bf16[768,2,5632]{2,0,1:T(8,128)(2,1)}), bf16[768,2,5632]{2,0,1:T(8,128)(2,1)}, u32[]{:S(2)}, u32[]{:S(2)}) async-start(bf16[768,2,5632]{2,0,1:T(8,128)(2,1)} %all-gather.5.cloned.1.call-done), calls=%async_computation.2 | async-start | bytes 34603008 | tf_op jit(solution)/shard_map/all_to_all | solution.py:129
  151.5 54.5 %all-gather.3.cloned.1.call-start = ((), (), s32[]{:S(2)}) async-start(), calls=%async_computation.3 | async-start | bytes 2359296 | tf_op jit(solution)/shard_map/all_gather | solution.py:107
  151.6 4.9 copy-start.11
  151.6 5.2 copy-start.7
  151.6 205.3 %copy-start.9 = (f32[1536]{0:T(1024)S(1)}, f32[1536]{0:T(1024)}, u32[]{:S(2)}) copy-start(f32[1536]{0:T(1024)} %param.14) | copy-start | bytes 18436
  156.3 286.6 %all-reduce.3.cloned.1.call-start = ((), (), s32[]{:S(2)}) async-start(), calls=%async_computation.5 | async-start | bytes 3145728 | tf_op jit(solution)/shard_map/psum | solution.py:150
  362.0 2.2 copy-start.3
  364.2 4.1 slice-start
  365.1 4.3 copy-start.4
  365.1 4.3 copy-start.5
  373.1 7.4 %copy-start.6 = (bf16[512,384]{0,1:T(8,128)(2,1)S(1)}, bf16[512,384]{0,1:T(8,128)(2,1)}, u32[]{:S(2)}) copy-start(bf16[512,384]{0,1:T(8,128)(2,1)} %copy.68) | copy-start | bytes 1179652
  387.3 58.3 %copy-start.10 = (f32[1536]{0:T(1024)S(1)}, f32[1536]{0:T(1024)}, u32[]{:S(2)}) copy-start(f32[1536]{0:T(1024)} %param.17) | copy-start | bytes 18436
  387.3 131.0 %all-reduce.5.cloned.1.call-start = ((), (), s32[]{:S(2)}) async-start(), calls=%async_computation.6 | async-start | bytes 3145728 | tf_op jit(solution)/shard_map/psum | solution.py:156
  442.9 2.6 copy-start.1
  442.9 2.8 copy-start.2
  442.9 14.9 %slice-start.1 = ((s8[6291456]{0:T(1024)(128)(4,1)}), s8[4194304]{0:T(1024)(128)(4,1)S(1)}, s32[]{:S(2)}) async-start(s8[6291456]{0:T(1024)(128)(4,1)} %bitcast.128), calls=%async_computation.8 | async-start | bytes 8388608
  445.7 12.1 %slice-start.2 = ((s8[6291456]{0:T(1024)(128)(4,1)}), s8[2097152]{0:T(1024)(128)(4,1)S(1)}, s32[]{:S(2)}) async-start(s8[6291456]{0:T(1024)(128)(4,1)} %bitcast.128), calls=%async_computation.9 | async-start | bytes 4194304
Sparse Core Ops, SparseCore 0:
  19.6 122.0 all-gather.4
Sparse Core Ops, SparseCore 1:
  156.4 49.6 all-gather.2
  387.4 55.5 all-reduce.2
  467.0 51.2 all-reduce.4
where the time goes:
time: 531 us; the launch traced here: 530 us
  waiting for transfers between devices  325 us (61%)
  blocking collectives  73.7 us (14%)
  local copies, waits for them, and re-layouts  41.4 us (8%)
  matrix products  40.4 us (8%)
  other arithmetic  22.7 us (4%)
  between operations  15.9 us (3%)
  starting transfers between devices  10.4 us (2%)
    all_to_all x1, waiting for transfers between devices, per_device(): lax.all_to_all(collected, 'tp', split_axis=1, concat_axis=0, tiled=True)  149 us
    all_to_all x1, blocking collectives, per_device(): lax.all_to_all(found_rows, 'req', split_axis=0, concat_axis=0, tiled=True)  60 us
    psum x1, waiting for transfers between devices, per_device(): lax.psum(jnp.dot(attended, out_weight, preferred_element_type=jnp.float32...  55.3 us
    psum x1, waiting for transfers between devices, per_device(): lax.psum(jnp.dot(hidden, down_weight, preferred_element_type=jnp.float32)...  49 us
    all_gather x1, waiting for transfers between devices, per_device(): lax.all_gather(returned[owner_of, slot_of], 'tp', axis=0, tiled=True)  47.1 us
    all_gather x1, waiting for transfers between devices, per_device(): collected = lax.all_gather(packed_rows, 'req', axis=0, tiled=True)  25 us
    all_to_all x1, blocking collectives, per_device(): lax.all_to_all(requests, 'req', split_axis=0, concat_axis=0, tiled=True)  13.7 us
    scatter x1, local copies, waits for them, and re-layouts, per_device(): jnp.full((group_count, capacity), -1, jnp.int32).at[owner_of, slot_of]  12.8 us
  transfers between devices with their start and end apart: 5, of which 5 were waited for; matrix products, arithmetic and copies ran while one was open for 7% of the time, Pallas kernels for 0%

commit v1 on v0

--- a/solution.py
+++ b/solution.py
@@ -125,7 +125,12 @@
         ],
         axis=2,
     )
-    collected = lax.all_gather(packed_rows, "req", axis=0, tiled=True)
+    ring = [packed_rows]
+    for hop in range(15):
+        ring.append(lax.ppermute(ring[-1], "req", [(dev, (dev + 1) % 16) for dev in range(16)]))
+    collected = jnp.roll(
+        jnp.concatenate(ring[::-1], axis=0), (lax.axis_index("req") + 1) * ring[0].shape[0], axis=0
+    )
     columns = lax.all_to_all(collected, "tp", split_axis=1, concat_axis=0, tiled=True)
     weights = columns[:, 0, :]
     normed = rms_scaled(embedded.astype(jnp.float32), attention_gain)

time: 531 us -> 740 us (1.39)
  waiting for transfers between devices: 325 us -> 538 us
  blocking collectives: 73.7 us -> 0 us
  local copies, waits for them, and re-layouts: 41.4 us -> 102 us
  starting transfers between devices: 10.4 us -> 21.9 us
    ppermute x0 -> x15, waiting for transfers between devices: none -> 225 us  [per_device(): lax.ppermute(ring[-1], 'req', [(dev, (dev + 1) % 16) for dev in range(16)])]
    all_to_all x2 -> x0, blocking collectives: 73.7 us -> none  [the longest x1 60 us: per_device(): lax.all_to_all(found_rows, 'req', split_axis=0, concat_axis=0, tiled=True)]
    unnamed x28 -> x109, local copies, waits for them, and re-layouts: 1 us -> 29.4 us
    all_gather x1 -> x0, waiting for transfers between devices: 25 us -> none  [per_device(): collected = lax.all_gather(packed_rows, 'req', axis=0, tiled=True)]
    scatter x1, local copies, waits for them, and re-layouts: 12.8 us -> 35.5 us  [per_device(): jnp.full((group_count, capacity), -1, jnp.int32).at[owner_of, slot_of]]
    all_to_all x0 -> x2, waiting for transfers between devices: none -> 12.2 us  [the longest x1 6.32 us: per_device(): lax.all_to_all(found_rows, 'req', split_axis=0, concat_axis=0, tiled=True)]
    all_to_all x0 -> x2, starting transfers between devices: none -> 10.4 us  [the longest x1 5.85 us: per_device(): lax.all_to_all(requests, 'req', split_axis=0, concat_axis=0, tiled=True)]
    dynamic_slice x0 -> x1, local copies, waits for them, and re-layouts: none -> 8.52 us  [per_device(): jnp.roll(jnp.concatenate(ring[::-1], axis=0), (lax.axis_index('req') + 1)...]
  transfers between devices with their start and end apart: 5 -> 21, of which waited for: 5 -> 19; matrix products, arithmetic and copies ran while one was open for 7% -> 11% of each run, Pallas kernels for 0% -> 0%
where the time goes in v1:
time: 740 us; the launch traced here: 738 us
  waiting for transfers between devices  538 us (73%)
  local copies, waits for them, and re-layouts  102 us (14%)
  matrix products  37.3 us (5%)
  other arithmetic  23.8 us (3%)
  starting transfers between devices  21.9 us (3%)
  between operations  14.4 us (2%)
    ppermute x15, waiting for transfers between devices, per_device(): lax.ppermute(ring[-1], 'req', [(dev, (dev + 1) % 16) for dev in range(16)])  225 us
    all_to_all x1, waiting for transfers between devices, per_device(): lax.all_to_all(collected, 'tp', split_axis=1, concat_axis=0, tiled=True)  150 us
    psum x1, waiting for transfers between devices, per_device(): lax.psum(jnp.dot(attended, out_weight, preferred_element_type=jnp.float32...  54.5 us
    psum x1, waiting for transfers between devices, per_device(): lax.psum(jnp.dot(hidden, down_weight, preferred_element_type=jnp.float32)...  49.2 us
    all_gather x1, waiting for transfers between devices, per_device(): lax.all_gather(returned[owner_of, slot_of], 'tp', axis=0, tiled=True)  46.8 us
    scatter x1, local copies, waits for them, and re-layouts, per_device(): jnp.full((group_count, capacity), -1, jnp.int32).at[owner_of, slot_of]  35.5 us
    unnamed x109, local copies, waits for them, and re-layouts  29.4 us
  transfers between devices with their start and end apart: 21, of which 19 were waited for; matrix products, arithmetic and copies ran while one was open for 11% of the time, Pallas kernels for 0%

profile of v1, /device:TPU:0, one launch (start us, length us, event | category | flops | bytes accessed | tf_op | source)
XLA Modules:
  0.0 737.9 jit_solution(10235592322297061293)
XLA Ops:
  19.6 17.8 %collective-permute-done = bf16[48,2,5632]{2,0,1:T(8,128)(2,1)S(1)} collective-permute-done((bf16[48,2,5632]{2,0,1:T(8,128)(2,1)S(1)}, bf16[48,2,5632]{2,0,1:T(8,128)(2,1)S(1)}, u32[]{:S(2)}, u32[]{:S(2)}) %collective-permute-start) | collective-permute-done | bytes 1081376 | tf_op jit(solution)/shard_map/ppermute | solution.py:130
  38.4 17.3 %collective-permute-done.1 = bf16[48,2,5632]{2,0,1:T(8,128)(2,1)S(1)} collective-permute-done((bf16[48,2,5632]{2,0,1:T(8,128)(2,1)S(1)}, bf16[48,2,5632]{2,0,1:T(8,128)(2,1)S(1)}, u32[]{:S(2)}, u32[]{:S(2)}) %collective-permute-start.1) | collective-permute-done | bytes 1081376 | tf_op jit(solution)/shard_map/ppermute | solution.py:130
  56.7 17.3 %collective-permute-done.2 = bf16[48,2,5632]{2,0,1:T(8,128)(2,1)S(1)} collective-permute-done((bf16[48,2,5632]{2,0,1:T(8,128)(2,1)S(1)}, bf16[48,2,5632]{2,0,1:T(8,128)(2,1)S(1)}, u32[]{:S(2)}, u32[]{:S(2)}) %collective-permute-start.2) | collective-permute-done | bytes 1081376 | tf_op jit(solution)/shard_map/ppermute | solution.py:130
  74.9 17.3 %collective-permute-done.3 = bf16[48,2,5632]{2,0,1:T(8,128)(2,1)S(1)} collective-permute-done((bf16[48,2,5632]{2,0,1:T(8,128)(2,1)S(1)}, bf16[48,2,5632]{2,0,1:T(8,128)(2,1)S(1)}, u32[]{:S(2)}, u32[]{:S(2)}) %collective-permute-start.3) | collective-permute-done | bytes 1081376 | tf_op jit(solution)/shard_map/ppermute | solution.py:130
  93.2 17.3 %collective-permute-done.4 = bf16[48,2,5632]{2,0,1:T(8,128)(2,1)S(1)} collective-permute-done((bf16[48,2,5632]{2,0,1:T(8,128)(2,1)S(1)}, bf16[48,2,5632]{2,0,1:T(8,128)(2,1)S(1)}, u32[]{:S(2)}, u32[]{:S(2)}) %collective-permute-start.4) | collective-permute-done | bytes 1081376 | tf_op jit(solution)/shard_map/ppermute | solution.py:130
  111.6 17.3 %collective-permute-done.5 = bf16[48,2,5632]{2,0,1:T(8,128)(2,1)S(1)} collective-permute-done((bf16[48,2,5632]{2,0,1:T(8,128)(2,1)S(1)}, bf16[48,2,5632]{2,0,1:T(8,128)(2,1)S(1)}, u32[]{:S(2)}, u32[]{:S(2)}) %collective-permute-start.5) | collective-permute-done | bytes 1081376 | tf_op jit(solution)/shard_map/ppermute | solution.py:130
  129.8 17.3 %collective-permute-done.6 = bf16[48,2,5632]{2,0,1:T(8,128)(2,1)S(1)} collective-permute-done((bf16[48,2,5632]{2,0,1:T(8,128)(2,1)S(1)}, bf16[48,2,5632]{2,0,1:T(8,128)(2,1)S(1)}, u32[]{:S(2)}, u32[]{:S(2)}) %collective-permute-start.6) | collective-permute-done | bytes 1081376 | tf_op jit(solution)/shard_map/ppermute | solution.py:130
  148.2 17.3 %collective-permute-done.7 = bf16[48,2,5632]{2,0,1:T(8,128)(2,1)S(1)} collective-permute-done((bf16[48,2,5632]{2,0,1:T(8,128)(2,1)S(1)}, bf16[48,2,5632]{2,0,1:T(8,128)(2,1)S(1)}, u32[]{:S(2)}, u32[]{:S(2)}) %collective-permute-start.7) | collective-permute-done | bytes 1081376 | tf_op jit(solution)/shard_map/ppermute | solution.py:130
  166.4 17.3 %collective-permute-done.8 = bf16[48,2,5632]{2,0,1:T(8,128)(2,1)S(1)} collective-permute-done((bf16[48,2,5632]{2,0,1:T(8,128)(2,1)S(1)}, bf16[48,2,5632]{2,0,1:T(8,128)(2,1)S(1)}, u32[]{:S(2)}, u32[]{:S(2)}) %collective-permute-start.8) | collective-permute-done | bytes 1081376 | tf_op jit(solution)/shard_map/ppermute | solution.py:130
  184.7 17.3 %collective-permute-done.9 = bf16[48,2,5632]{2,0,1:T(8,128)(2,1)S(1)} collective-permute-done((bf16[48,2,5632]{2,0,1:T(8,128)(2,1)S(1)}, bf16[48,2,5632]{2,0,1:T(8,128)(2,1)S(1)}, u32[]{:S(2)}, u32[]{:S(2)}) %collective-permute-start.9) | collective-permute-done | bytes 1081376 | tf_op jit(solution)/shard_map/ppermute | solution.py:130
  203.0 17.3 %collective-permute-done.10 = bf16[48,2,5632]{2,0,1:T(8,128)(2,1)S(1)} collective-permute-done((bf16[48,2,5632]{2,0,1:T(8,128)(2,1)S(1)}, bf16[48,2,5632]{2,0,1:T(8,128)(2,1)S(1)}, u32[]{:S(2)}, u32[]{:S(2)}) %collective-permute-start.10) | collective-permute-done | bytes 1081376 | tf_op jit(solution)/shard_map/ppermute | solution.py:130
  221.3 17.3 %collective-permute-done.11 = bf16[48,2,5632]{2,0,1:T(8,128)(2,1)S(1)} collective-permute-done((bf16[48,2,5632]{2,0,1:T(8,128)(2,1)S(1)}, bf16[48,2,5632]{2,0,1:T(8,128)(2,1)S(1)}, u32[]{:S(2)}, u32[]{:S(2)}) %collective-permute-start.11) | collective-permute-done | bytes 1081376 | tf_op jit(solution)/shard_map/ppermute | solution.py:130
  239.6 17.4 %collective-permute-done.12 = bf16[48,2,5632]{2,0,1:T(8,128)(2,1)} collective-permute-done((bf16[48,2,5632]{2,0,1:T(8,128)(2,1)S(1)}, bf16[48,2,5632]{2,0,1:T(8,128)(2,1)}, u32[]{:S(2)}, u32[]{:S(2)}) %collective-permute-start.12) | collective-permute-done | bytes 1081376 | tf_op jit(solution)/shard_map/ppermute | solution.py:130
  258.6 35.5 %scatter_fusion = s32[16,32]{1,0:T(8,128)} fusion(s32[16,32]{1,0:T(8,128)} %broadcast_in_dim.22, s32[256]{0:T(256)S(1)} %bitcast.118, s32[256]{0:T(256)S(1)} %get-tuple-element.4), kind=kCustom, calls=%fused_computation.2 | custom fusion | bytes 5120 | tf_op jit(solution)/shard_map/scatter | solution.py:99
  294.1 5.8 all-to-all-start
  300.4 5.9 all-to-all-done
  306.4 7.9 %gather_fusion = bf16[512,1536]{1,0:T(8,128)(2,1)} fusion(bf16[2000,1536]{1,0:T(8,128)(2,1)} %param.13, s32[1024]{0:T(1024)S(1)} %pad_clamp_fusion), kind=kCustom, calls=%fused_computation | custom fusion | bytes 3147776 | tf_op jit(solution)/shard_map/jit(_take)/gather | solution.py:101
  317.1 4.6 all-to-all-start.1
  338.7 8.5 %constant_dynamic-slice_fusion = bf16[768,2,5632]{2,0,1:T(8,128)(2,1)} fusion(bf16[1536,2,5632]{2,0,1:T(8,128)(2,1)S(1)} %constant_dynamic-update-slice_fusion, s32[]{:T(128)S(6)} %select_n.53), kind=kLoop, calls=%fused_computation.126 | loop fusion | bytes 34603012 | tf_op jit(solution)/shard_map/jit(_roll_dynamic)/dynamic_slice | solution.py:131
  347.2 6.3 all-to-all-done.1
  353.5 9.9 %all-to-all-start.2 = ((bf16[768,2,5632]{2,0,1:T(8,128)(2,1)}), bf16[768,2,5632]{2,0,1:T(8,128)(2,1)}, u32[]{:S(2)}, u32[]{:S(2)}) async-start(bf16[768,2,5632]{2,0,1:T(8,128)(2,1)} %constant_dynamic-slice_fusion), calls=%async_computation.2 | async-start | bytes 34603008 | tf_op jit(solution)/shard_map/all_to_all | solution.py:134
  363.5 4.6 gather_fusion.1
  370.9 46.8 %all-gather.2.cloned.1.call-done = bf16[512,1536]{1,0:T(8,128)(2,1)} async-done(((bf16[256,1536]{1,0:T(8,128)(2,1)}), bf16[512,1536]{1,0:T(8,128)(2,1)}) %all-gather.2.cloned.1.call-update) | async-done | bytes 1572880 | tf_op jit(solution)/shard_map/all_gather | solution.py:107
  419.5 150.2 %all-to-all-done.2 = bf16[768,2,5632]{2,0,1:T(8,128)(2,1)} async-done(((bf16[768,2,5632]{2,0,1:T(8,128)(2,1)}), bf16[768,2,5632]{2,0,1:T(8,128)(2,1)}, u32[]{:S(2)}, u32[]{:S(2)}) %all-to-all-start.2) | async-done | bytes 17301536 | tf_op jit(solution)/shard_map/all_to_all | solution.py:134
  569.7 5.0 fusion.4
  586.0 7.5 %fusion.44 = (f32[4,2,512]{2,1,0:T(2,128)S(1)}, f32[4,2,512,512]{2,3,1,0:T(8,128)}) fusion(pred[512,512]{0,1:T(8,128)(4,1)} %fusion.21, bf16[512,4,2,48]{0,3,2,1:T(8,128)(2,1)} %bitcast.136, bf16[512,4,2,48]{0,3,2,1:T(8,128)(2,1)S(1)} %bitcast.135, bf16[512,4,48]{0,2,1:T(8,128)(2,1)S(1)} %get-tuple-element.11, bf16[512,4,48]{0,2,1:T(8,128)(2,1)S(1)} %get-tuple-element.10), kind=kOutput, calls=%fused_computation.132 | convolution fusion | flops 413401600 | bytes 9846784 | tf_op jit(solution)/shard_map/sub | solution.py:58
  593.4 4.2 fusion.20
  600.6 54.5 %all-reduce.3.cloned.1.call-done = bf16[512,1536]{1,0:T(8,128)(2,1)} async-done(((bf16[512,1536]{1,0:T(8,128)(2,1)}), bf16[512,1536]{1,0:T(8,128)(2,1)}) %all-reduce.3.cloned.1.call-update) | async-done | bytes 1572880 | tf_op jit(solution)/shard_map/psum | solution.py:155
  657.5 10.7 %fusion.1 = f32[512,4096]{1,0:T(8,128)S(1)} fusion(bf16[1536,5632]{1,0:T(8,128)(2,1)} %bitcast.14, bf16[512,1536]{1,0:T(8,128)(2,1)} %all-reduce.3.cloned.1.call-done, bf16[512,1536]{1,0:T(8,128)(2,1)} %all-gather.2.cloned.1.call-done, f32[1536]{0:T(1024)S(1)} %copy-done.34, f32[512]{0:T(512)S(1)} %add_rsqrt_fusion), kind=kOutput, calls=%fused_computation.4 | convolution fusion | flops 6447169536 | bytes 24125440 | tf_op jit(solution)/shard_map/dot_general | solution.py:68
  668.2 7.4 %convolution_convert_fusion = bf16[512,1536]{1,0:T(8,128)(2,1)} fusion(bf16[2048,1536]{1,0:T(8,128)(2,1)} %param.19, f32[512,4096]{1,0:T(8,128)S(1)} %fusion.1), kind=kOutput, calls=%fused_computation.27 | convolution fusion | flops 3228303360 | bytes 16252928 | tf_op jit(solution)/shard_map/dot_general | solution.py:162
  678.1 49.2 %all-reduce.5.cloned.1.call-done = bf16[512,1536]{1,0:T(8,128)(2,1)} async-done(((bf16[512,1536]{1,0:T(8,128)(2,1)}), bf16[512,1536]{1,0:T(8,128)(2,1)}) %all-reduce.5.cloned.1.call-update) | async-done | bytes 1572880 | tf_op jit(solution)/shard_map/psum | solution.py:161
  727.3 4.1 add_convert_fusion
  (183 shorter events, 69.6 us)
Async XLA Ops:
  7.2 590.5 %copy-start = (bf16[768,1536]{1,0:T(8,128)(2,1)S(1)}, bf16[768,1536]{1,0:T(8,128)(2,1)}, u32[]{:S(2)}) copy-start(bf16[768,1536]{1,0:T(8,128)(2,1)} %param.16) | copy-start | bytes 7077892
  9.1 247.8 %copy-start.32 = (s32[512]{0:T(512)S(1)}, s32[512]{0:T(512)}, u32[]{:S(2)}) copy-start(s32[512]{0:T(512)} %param.10) | copy-start | bytes 6148
  19.1 18.3 %collective-permute-start = (bf16[48,2,5632]{2,0,1:T(8,128)(2,1)S(1)}, bf16[48,2,5632]{2,0,1:T(8,128)(2,1)S(1)}, u32[]{:S(2)}, u32[]{:S(2)}) collective-permute-start(bf16[48,2,5632]{2,0,1:T(8,128)(2,1)S(1)} %pad_maximum_fusion), channel_id=1, source_target_pairs={{0,1},{1,2},{2,3},{3,4},{4,5},{5,6},{6,7},{7,8},{8,9},{9,10},{10,1... | collective-permute-start | bytes 3244040 | tf_op jit(solution)/shard_map/ppermute | solution.py:130
  38.4 17.3 %collective-permute-start.1 = (bf16[48,2,5632]{2,0,1:T(8,128)(2,1)S(1)}, bf16[48,2,5632]{2,0,1:T(8,128)(2,1)S(1)}, u32[]{:S(2)}, u32[]{:S(2)}) collective-permute-start(bf16[48,2,5632]{2,0,1:T(8,128)(2,1)S(1)} %collective-permute-done), channel_id=1, source_target_pairs={{0,1},{1,2},{2,3},{3,4},{4,5},{5,6},{6,7},{7,8},{8,9},{9,10},{10,1... | collective-permute-start | bytes 3244040 | tf_op jit(solution)/shard_map/ppermute | solution.py:130
  56.7 17.3 %collective-permute-start.2 = (bf16[48,2,5632]{2,0,1:T(8,128)(2,1)S(1)}, bf16[48,2,5632]{2,0,1:T(8,128)(2,1)S(1)}, u32[]{:S(2)}, u32[]{:S(2)}) collective-permute-start(bf16[48,2,5632]{2,0,1:T(8,128)(2,1)S(1)} %collective-permute-done.1), channel_id=1, source_target_pairs={{0,1},{1,2},{2,3},{3,4},{4,5},{5,6},{6,7},{7,8},{8,9},{9,10},{10,1... | collective-permute-start | bytes 3244040 | tf_op jit(solution)/shard_map/ppermute | solution.py:130
  74.9 17.3 %collective-permute-start.3 = (bf16[48,2,5632]{2,0,1:T(8,128)(2,1)S(1)}, bf16[48,2,5632]{2,0,1:T(8,128)(2,1)S(1)}, u32[]{:S(2)}, u32[]{:S(2)}) collective-permute-start(bf16[48,2,5632]{2,0,1:T(8,128)(2,1)S(1)} %collective-permute-done.2), channel_id=1, source_target_pairs={{0,1},{1,2},{2,3},{3,4},{4,5},{5,6},{6,7},{7,8},{8,9},{9,10},{10,1... | collective-permute-start | bytes 3244040 | tf_op jit(solution)/shard_map/ppermute | solution.py:130
  93.2 17.3 %collective-permute-start.4 = (bf16[48,2,5632]{2,0,1:T(8,128)(2,1)S(1)}, bf16[48,2,5632]{2,0,1:T(8,128)(2,1)S(1)}, u32[]{:S(2)}, u32[]{:S(2)}) collective-permute-start(bf16[48,2,5632]{2,0,1:T(8,128)(2,1)S(1)} %collective-permute-done.3), channel_id=1, source_target_pairs={{0,1},{1,2},{2,3},{3,4},{4,5},{5,6},{6,7},{7,8},{8,9},{9,10},{10,1... | collective-permute-start | bytes 3244040 | tf_op jit(solution)/shard_map/ppermute | solution.py:130
  111.6 17.3 %collective-permute-start.5 = (bf16[48,2,5632]{2,0,1:T(8,128)(2,1)S(1)}, bf16[48,2,5632]{2,0,1:T(8,128)(2,1)S(1)}, u32[]{:S(2)}, u32[]{:S(2)}) collective-permute-start(bf16[48,2,5632]{2,0,1:T(8,128)(2,1)S(1)} %collective-permute-done.4), channel_id=1, source_target_pairs={{0,1},{1,2},{2,3},{3,4},{4,5},{5,6},{6,7},{7,8},{8,9},{9,10},{10,1... | collective-permute-start | bytes 3244040 | tf_op jit(solution)/shard_map/ppermute | solution.py:130
  129.8 17.3 %collective-permute-start.6 = (bf16[48,2,5632]{2,0,1:T(8,128)(2,1)S(1)}, bf16[48,2,5632]{2,0,1:T(8,128)(2,1)S(1)}, u32[]{:S(2)}, u32[]{:S(2)}) collective-permute-start(bf16[48,2,5632]{2,0,1:T(8,128)(2,1)S(1)} %collective-permute-done.5), channel_id=1, source_target_pairs={{0,1},{1,2},{2,3},{3,4},{4,5},{5,6},{6,7},{7,8},{8,9},{9,10},{10,1... | collective-permute-start | bytes 3244040 | tf_op jit(solution)/shard_map/ppermute | solution.py:130
  148.2 17.3 %collective-permute-start.7 = (bf16[48,2,5632]{2,0,1:T(8,128)(2,1)S(1)}, bf16[48,2,5632]{2,0,1:T(8,128)(2,1)S(1)}, u32[]{:S(2)}, u32[]{:S(2)}) collective-permute-start(bf16[48,2,5632]{2,0,1:T(8,128)(2,1)S(1)} %collective-permute-done.6), channel_id=1, source_target_pairs={{0,1},{1,2},{2,3},{3,4},{4,5},{5,6},{6,7},{7,8},{8,9},{9,10},{10,1... | collective-permute-start | bytes 3244040 | tf_op jit(solution)/shard_map/ppermute | solution.py:130
  166.4 17.3 %collective-permute-start.8 = (bf16[48,2,5632]{2,0,1:T(8,128)(2,1)S(1)}, bf16[48,2,5632]{2,0,1:T(8,128)(2,1)S(1)}, u32[]{:S(2)}, u32[]{:S(2)}) collective-permute-start(bf16[48,2,5632]{2,0,1:T(8,128)(2,1)S(1)} %collective-permute-done.7), channel_id=1, source_target_pairs={{0,1},{1,2},{2,3},{3,4},{4,5},{5,6},{6,7},{7,8},{8,9},{9,10},{10,1... | collective-permute-start | bytes 3244040 | tf_op jit(solution)/shard_map/ppermute | solution.py:130
  184.7 17.3 %collective-permute-start.9 = (bf16[48,2,5632]{2,0,1:T(8,128)(2,1)S(1)}, bf16[48,2,5632]{2,0,1:T(8,128)(2,1)S(1)}, u32[]{:S(2)}, u32[]{:S(2)}) collective-permute-start(bf16[48,2,5632]{2,0,1:T(8,128)(2,1)S(1)} %collective-permute-done.8), channel_id=1, source_target_pairs={{0,1},{1,2},{2,3},{3,4},{4,5},{5,6},{6,7},{7,8},{8,9},{9,10},{10,1... | collective-permute-start | bytes 3244040 | tf_op jit(solution)/shard_map/ppermute | solution.py:130
  203.0 17.3 %collective-permute-start.10 = (bf16[48,2,5632]{2,0,1:T(8,128)(2,1)S(1)}, bf16[48,2,5632]{2,0,1:T(8,128)(2,1)S(1)}, u32[]{:S(2)}, u32[]{:S(2)}) collective-permute-start(bf16[48,2,5632]{2,0,1:T(8,128)(2,1)S(1)} %collective-permute-done.9), channel_id=1, source_target_pairs={{0,1},{1,2},{2,3},{3,4},{4,5},{5,6},{6,7},{7,8},{8,9},{9,10},{10,1... | collective-permute-start | bytes 3244040 | tf_op jit(solution)/shard_map/ppermute | solution.py:130
  221.3 17.3 %collective-permute-start.11 = (bf16[48,2,5632]{2,0,1:T(8,128)(2,1)S(1)}, bf16[48,2,5632]{2,0,1:T(8,128)(2,1)S(1)}, u32[]{:S(2)}, u32[]{:S(2)}) collective-permute-start(bf16[48,2,5632]{2,0,1:T(8,128)(2,1)S(1)} %collective-permute-done.10), channel_id=1, source_target_pairs={{0,1},{1,2},{2,3},{3,4},{4,5},{5,6},{6,7},{7,8},{8,9},{9,10},{10,1... | collective-permute-start | bytes 3244040 | tf_op jit(solution)/shard_map/ppermute | solution.py:130
  239.6 17.4 %collective-permute-start.12 = (bf16[48,2,5632]{2,0,1:T(8,128)(2,1)S(1)}, bf16[48,2,5632]{2,0,1:T(8,128)(2,1)}, u32[]{:S(2)}, u32[]{:S(2)}) collective-permute-start(bf16[48,2,5632]{2,0,1:T(8,128)(2,1)S(1)} %collective-permute-done.11), channel_id=1, source_target_pairs={{0,1},{1,2},{2,3},{3,4},{4,5},{5,6},{6,7},{7,8},{8,9},{9,10},{10,1... | collective-permute-start | bytes 3244040 | tf_op jit(solution)/shard_map/ppermute | solution.py:130
  256.9 43.0 %collective-permute-start.13 = (bf16[48,2,5632]{2,0,1:T(8,128)(2,1)}, bf16[48,2,5632]{2,0,1:T(8,128)(2,1)}, u32[]{:S(2)}, u32[]{:S(2)}) collective-permute-start(bf16[48,2,5632]{2,0,1:T(8,128)(2,1)} %collective-permute-done.12), channel_id=1, source_target_pairs={{0,1},{1,2},{2,3},{3,4},{4,5},{5,6},{6,7},{7,8},{8,9},{9,10},{10,1... | collective-permute-start | bytes 3244040 | tf_op jit(solution)/shard_map/ppermute | solution.py:130
  294.1 12.2 %all-to-all-start = ((s32[16,1,32]{2,1,0:T(1,128)}), s32[16,1,32]{2,1,0:T(1,128)S(1)}, u32[]{:S(2)}, u32[]{:S(2)}) async-start(s32[16,1,32]{2,1,0:T(1,128)} %bitcast.6), calls=%async_computation | async-start | bytes 16384 | tf_op jit(solution)/shard_map/all_to_all | solution.py:103
  300.0 21.8 %collective-permute-start.14 = (bf16[48,2,5632]{2,0,1:T(8,128)(2,1)}, bf16[48,2,5632]{2,0,1:T(8,128)(2,1)}, u32[]{:S(2)}, u32[]{:S(2)}) collective-permute-start(bf16[48,2,5632]{2,0,1:T(8,128)(2,1)} %collective-permute-done.13), channel_id=1, source_target_pairs={{0,1},{1,2},{2,3},{3,4},{4,5},{5,6},{6,7},{7,8},{8,9},{9,10},{10,1... | collective-permute-start | bytes 3244040 | tf_op jit(solution)/shard_map/ppermute | solution.py:130
  317.1 36.4 %all-to-all-start.1 = ((bf16[16,32,1536]{2,1,0:T(8,128)(2,1)}), bf16[16,32,1536]{2,1,0:T(8,128)(2,1)}, u32[]{:S(2)}, u32[]{:S(2)}) async-start(bf16[16,32,1536]{2,1,0:T(8,128)(2,1)} %broadcast_select_fusion), calls=%async_computation.1 | async-start | bytes 3145728 | tf_op jit(solution)/shard_map/all_to_all | solution.py:106
  353.5 216.2 %all-to-all-start.2 = ((bf16[768,2,5632]{2,0,1:T(8,128)(2,1)}), bf16[768,2,5632]{2,0,1:T(8,128)(2,1)}, u32[]{:S(2)}, u32[]{:S(2)}) async-start(bf16[768,2,5632]{2,0,1:T(8,128)(2,1)} %constant_dynamic-slice_fusion), calls=%async_computation.2 | async-start | bytes 34603008 | tf_op jit(solution)/shard_map/all_to_all | solution.py:134
  363.4 5.0 copy-start.35
  363.4 5.3 copy-start.31
  363.4 54.2 %all-gather.2.cloned.1.call-start = ((), (), s32[]{:S(2)}) async-start(), calls=%async_computation.3 | async-start | bytes 2359296 | tf_op jit(solution)/shard_map/all_gather | solution.py:107
  363.5 206.2 %copy-start.33 = (f32[1536]{0:T(1024)S(1)}, f32[1536]{0:T(1024)}, u32[]{:S(2)}) copy-start(f32[1536]{0:T(1024)} %param.14) | copy-start | bytes 18436
  368.2 286.9 %all-reduce.3.cloned.1.call-start = ((), (), s32[]{:S(2)}) async-start(), calls=%async_computation.4 | async-start | bytes 3145728 | tf_op jit(solution)/shard_map/psum | solution.py:155
  582.5 11.0 %copy-start.26 = (bf16[512,4,48]{0,2,1:T(8,128)(2,1)}, bf16[512,4,48]{0,2,1:T(8,128)(2,1)S(1)}, u32[]{:S(2)}) copy-start(bf16[512,4,48]{0,2,1:T(8,128)(2,1)S(1)} %get-tuple-element.10) | copy-start | bytes 589828
  582.5 11.0 %copy-start.28 = (bf16[512,4,48]{0,2,1:T(8,128)(2,1)}, bf16[512,4,48]{0,2,1:T(8,128)(2,1)S(1)}, u32[]{:S(2)}) copy-start(bf16[512,4,48]{0,2,1:T(8,128)(2,1)S(1)} %get-tuple-element.11) | copy-start | bytes 589828
  586.0 7.5 %copy-start.30 = (bf16[512,384]{0,1:T(8,128)(2,1)S(1)}, bf16[512,384]{0,1:T(8,128)(2,1)}, u32[]{:S(2)}) copy-start(bf16[512,384]{0,1:T(8,128)(2,1)} %copy.68) | copy-start | bytes 1179652
  597.6 59.9 %copy-start.34 = (f32[1536]{0:T(1024)S(1)}, f32[1536]{0:T(1024)}, u32[]{:S(2)}) copy-start(f32[1536]{0:T(1024)} %param.17) | copy-start | bytes 18436
  600.2 127.1 %all-reduce.5.cloned.1.call-start = ((), (), s32[]{:S(2)}) async-start(), calls=%async_computation.5 | async-start | bytes 3145728 | tf_op jit(solution)/shard_map/psum | solution.py:161
  668.2 7.4 %copy-start.27 = (bf16[512,4,48]{0,2,1:T(8,128)(2,1)S(1)}, bf16[512,4,48]{0,2,1:T(8,128)(2,1)}, u32[]{:S(2)}) copy-start(bf16[512,4,48]{0,2,1:T(8,128)(2,1)} %copy-done.26) | copy-start | bytes 589828
  668.2 7.4 %copy-start.29 = (bf16[512,4,48]{0,2,1:T(8,128)(2,1)S(1)}, bf16[512,4,48]{0,2,1:T(8,128)(2,1)}, u32[]{:S(2)}) copy-start(bf16[512,4,48]{0,2,1:T(8,128)(2,1)} %copy-done.28) | copy-start | bytes 589828
  (25 other events, 40.0 us)
Sparse Core Ops, SparseCore 0:
  368.3 49.3 all-gather.1
  600.4 54.6 all-reduce.2
  675.8 51.4 all-reduce.4
